TPU v7x, 32 devices: a whole 2x2x4 slice. The times are simulated.
32 devices in a mesh: group: 8 (over z, x), ctx: 2 (over y), wshard: 2 (over core).
Axes of the slice: x: 2, y: 2, z: 4, core: 2. Of those that a mesh axis runs over, the one named last changes fastest.
Arguments:
- inputs: bfloat16 [8192, 1536], P(('group', 'ctx', 'wshard')), may hold values from -6 to 6
- out_grad: bfloat16 [8192, 1536], P(('group', 'ctx', 'wshard')), may hold values from -6 to 6
- lengths: int32 [8, 4], P('group'), may hold values from 1 to 512, 1024 in all within a row
- permutation: int32 [8, 1024], P('group'), may hold values from 0 to 1023, each once within a row
- gain_attention: float32 [1536], replicated, may hold values from 0.5 to 1.5
- query_weight: bfloat16 [1536, 768], P('wshard'), may hold values from -0.0546875 to 0.0546875
- key_weight: bfloat16 [1536, 768], P('wshard'), may hold values from -0.0546875 to 0.0546875
- value_weight: bfloat16 [1536, 768], P('wshard'), may hold values from -0.15625 to 0.15625
- out_weight: bfloat16 [768, 1536], P('wshard'), may hold values from -3.5 to 3.5
- bucket_bias: float32 [32, 12], replicated, may hold values from -4 to 4
- gain_feedforward: float32 [1536], replicated, may hold values from 0.5 to 1.5
- gate_weight: bfloat16 [1536, 3968], P('wshard'), may hold values from -0.15625 to 0.15625
- up_weight: bfloat16 [1536, 3968], P('wshard'), may hold values from -0.15625 to 0.15625
- down_weight: bfloat16 [3968, 1536], P('wshard'), may hold values from -0.09375 to 0.09375
Outputs:
- outputs: bfloat16 [8192, 1536], P(('group', 'ctx', 'wshard'))
- input_grad: bfloat16 [8192, 1536], P(('group', 'ctx', 'wshard'))
- grad_gain_attention: float32 [1536], P(('ctx', 'wshard'))
- grad_query: float32 [1536, 768], P(('ctx', 'wshard'))
- grad_key: float32 [1536, 768], P(('ctx', 'wshard'))
- grad_value: float32 [1536, 768], P(('ctx', 'wshard'))
- grad_out: float32 [768, 1536], P(('ctx', 'wshard'))
- grad_bias: float32 [32, 12], replicated
- grad_gain_feedforward: float32 [1536], P(('ctx', 'wshard'))
- grad_gate: float32 [1536, 3968], P(('ctx', 'wshard'))
- grad_up: float32 [1536, 3968], P(('ctx', 'wshard'))
- grad_down: float32 [3968, 1536], P(None, ('ctx', 'wshard'))
Inputs may be any that keep to these rules, and one draw needn't show every extreme that they name: `lengths`: each row sums to 1024; the largest entry is 512. `permutation`: each row holds every place of its group once.
All inputs are finite; a program needn't handle non-finite values.
Results may differ from a plain program's by a relative error of at most 0.02.
Values may be sent and summed in bfloat16 or wider, within the bound.
No kernel may reach another device: no remote copies, remote signals or barrier semaphores. Data moves between devices by JAX's collectives and lax.ppermute only.
A program may use at most 320 MiB of HBM per device.

v0:
```python
import jax
import jax.numpy as jnp
from jax import lax
from jax.sharding import PartitionSpec as P

epsilon = 1e-06
highest = lax.Precision.HIGHEST
thresholds = (12, 16, 23, 32, 46, 64, 91)
masked_out = -1e30


def bucket_of(offset):
    distance = jnp.abs(offset)
    beyond = 8 + sum(((distance >= border).astype(jnp.int32) for border in thresholds))
    near_far = jnp.where(distance < 8, distance, beyond)
    return jnp.where(offset > 0, 16, 0) + near_far


def rms_norm(values, gain_vector):
    return (
        values
        * lax.rsqrt(jnp.mean(values * values, axis=-1, keepdims=True) + epsilon)
        * gain_vector
    )


def forward_product(left_side, right_side):
    return jnp.dot(left_side, right_side, preferred_element_type=jnp.float32)


def backward_product(left_side, right_side):
    return lax.dot_general(
        left_side, right_side, (((1,), (1,)), ((), ())), preferred_element_type=jnp.float32
    )


def weight_product(left_side, right_side):
    return lax.dot_general(
        left_side, right_side, (((0,), (0,)), ((), ())), preferred_element_type=jnp.float32
    )


def per_device(
    inputs,
    out_grad,
    lengths,
    permutation,
    gain_attention,
    query_weight,
    key_weight,
    value_weight,
    out_weight,
    bucket_bias,
    gain_feedforward,
    gate_weight,
    up_weight,
    down_weight,
):
    gathered = (
        lax.all_gather(query_weight, "wshard", axis=0, tiled=True),
        lax.all_gather(key_weight, "wshard", axis=0, tiled=True),
        lax.all_gather(value_weight, "wshard", axis=0, tiled=True),
        lax.all_gather(out_weight, "wshard", axis=0, tiled=True),
        lax.all_gather(gate_weight, "wshard", axis=0, tiled=True),
        lax.all_gather(up_weight, "wshard", axis=0, tiled=True),
        lax.all_gather(down_weight, "wshard", axis=0, tiled=True),
    )
    query_full, key_full, value_full, out_full, gate_full, up_full, down_full = gathered
    rows = inputs.shape[0]
    buckets = bucket_bias.shape[0]
    heads = bucket_bias.shape[1]
    width = query_weight.shape[1]
    head_size = width // heads
    peers = lax.axis_size(("ctx", "wshard"))
    group_tokens = rows * peers
    breadth = min(512, group_tokens)
    blocks = group_tokens // breadth
    first = lax.axis_index(("ctx", "wshard")) * rows
    seq_ends = jnp.cumsum(lengths[0])
    order_row = permutation[0]
    inverse = (
        jnp.zeros((group_tokens,), jnp.int32).at[order_row].set(lax.iota(jnp.int32, group_tokens))
    )

    def sequence_of(places):
        return jnp.sum((places[:, None] >= seq_ends[None, :]).astype(jnp.int32), axis=1)

    query_place = lax.dynamic_slice_in_dim(order_row, first, rows, 0)
    query_seq = sequence_of(query_place)
    seq_lowest = jnp.min(query_seq)
    seq_highest = jnp.max(query_seq)
    bucket_ids = lax.iota(jnp.int32, buckets)

    def live(key_start):
        key_seq = sequence_of(lax.dynamic_slice_in_dim(order_row, key_start, breadth, 0))
        return (jnp.min(key_seq) <= seq_highest) & (jnp.max(key_seq) >= seq_lowest)

    all_grads = lax.all_gather(out_grad, ("ctx", "wshard"), axis=0, tiled=True)
    dy_rows = jnp.take(all_grads, query_place, axis=0)
    inputs_wide = inputs.astype(jnp.float32)
    normed = rms_norm(inputs_wide, gain_attention).astype(jnp.bfloat16)
    query_proj = forward_product(normed, query_full).astype(jnp.bfloat16)
    key_proj = forward_product(normed, key_full).astype(jnp.bfloat16)
    value_proj = forward_product(normed, value_full).astype(jnp.bfloat16)
    query_heads = query_proj.reshape(rows, heads, head_size)
    key_value = (
        lax.all_gather(key_proj, ("ctx", "wshard"), axis=0, tiled=True),
        lax.all_gather(value_proj, ("ctx", "wshard"), axis=0, tiled=True),
    )

    def block_scores(key_start, key_all):
        key_block = lax.dynamic_slice_in_dim(key_all, key_start, breadth, 0).reshape(
            breadth, heads, head_size
        )
        scores = jnp.einsum(
            "qhd,khd->hqk", query_heads, key_block, preferred_element_type=jnp.float32
        )
        key_place = lax.dynamic_slice_in_dim(order_row, key_start, breadth, 0)
        offsets = key_place[None, :] - query_place[:, None]
        picks = (bucket_of(offsets)[:, :, None] == bucket_ids[None, None, :]).astype(jnp.float32)
        scores = scores + jnp.einsum("qkb,bh->hqk", picks, bucket_bias, precision=highest)
        key_seq = sequence_of(key_place)
        same_seq = (query_seq[:, None] == key_seq[None, :])[None]
        return (jnp.where(same_seq, scores, masked_out), key_block, picks)

    def value_block_of(key_start, value_all):
        return lax.dynamic_slice_in_dim(value_all, key_start, breadth, 0).reshape(
            breadth, heads, head_size
        )

    def visit(step_fn, carry):

        def one_step(block_index, running):
            key_start = block_index * breadth
            return lax.cond(
                live(key_start),
                lambda current: step_fn(key_start, current),
                lambda current: current,
                running,
            )

        return lax.fori_loop(0, blocks, one_step, carry)

    def peak_step(key_start, running):
        top_now, total_now = running
        scores = block_scores(key_start, key_value[0])[0]
        top_next = jnp.maximum(top_now, jnp.max(scores, axis=2))
        total_next = total_now * jnp.exp(top_now - top_next) + jnp.sum(
            jnp.exp(scores - top_next[:, :, None]), axis=2
        )
        return (top_next, total_next)

    start_top = jnp.full((heads, rows), masked_out, jnp.float32)
    top_all, total_all = visit(peak_step, (start_top, jnp.zeros((heads, rows), jnp.float32)))
    log_total = top_all + jnp.log(total_all)

    def value_step(key_start, running):
        scores = block_scores(key_start, key_value[0])[0]
        value_block = value_block_of(key_start, key_value[1])
        probs_low = jnp.exp(scores - log_total[:, :, None]).astype(jnp.bfloat16)
        return running + jnp.einsum(
            "hqk,khd->qhd", probs_low, value_block, preferred_element_type=jnp.float32
        )

    attended_wide = visit(value_step, jnp.zeros((rows, heads, head_size), jnp.float32))
    attended = attended_wide.reshape(rows, width).astype(jnp.bfloat16)
    residual = inputs_wide + forward_product(attended, out_full)
    normed_ff = rms_norm(residual, gain_feedforward).astype(jnp.bfloat16)
    gate_proj = forward_product(normed_ff, gate_full)
    up_proj = forward_product(normed_ff, up_full)

    def activate(gate_in, up_in):
        return jax.nn.gelu(gate_in, approximate=True) * up_in

    hidden_wide, activate_back = jax.vjp(activate, gate_proj, up_proj)
    hidden = hidden_wide.astype(jnp.bfloat16)
    outputs_dealt = (residual + forward_product(hidden, down_full)).astype(jnp.bfloat16)
    later = (
        lax.all_gather(query_weight, "wshard", axis=0, tiled=True),
        lax.all_gather(key_weight, "wshard", axis=0, tiled=True),
        lax.all_gather(value_weight, "wshard", axis=0, tiled=True),
        lax.all_gather(out_weight, "wshard", axis=0, tiled=True),
        lax.all_gather(gate_weight, "wshard", axis=0, tiled=True),
        lax.all_gather(up_weight, "wshard", axis=0, tiled=True),
        lax.all_gather(down_weight, "wshard", axis=0, tiled=True),
    )
    key_value_back = (
        lax.all_gather(key_proj, ("ctx", "wshard"), axis=0, tiled=True),
        lax.all_gather(value_proj, ("ctx", "wshard"), axis=0, tiled=True),
    )
    query_back, key_back, value_back, out_back, gate_back, up_back, down_back = later
    grad_down = weight_product(hidden, dy_rows)
    d_hidden = backward_product(dy_rows, down_back)
    d_gate_wide, d_up_wide = activate_back(d_hidden)
    d_gate = d_gate_wide.astype(jnp.bfloat16)
    d_up = d_up_wide.astype(jnp.bfloat16)
    grad_gate = weight_product(normed_ff, d_gate)
    grad_up = weight_product(normed_ff, d_up)
    d_normed_ff = backward_product(d_gate, gate_back) + backward_product(d_up, up_back)
    norm_ff_back = jax.vjp(rms_norm, residual, gain_feedforward)[1]
    d_residual_norm, grad_gain_ff = norm_ff_back(d_normed_ff)
    d_residual = dy_rows.astype(jnp.float32) + d_residual_norm
    d_branch = d_residual.astype(jnp.bfloat16)
    grad_out = weight_product(attended, d_branch)
    d_attended = backward_product(d_branch, out_back).astype(jnp.bfloat16)
    d_heads = d_attended.reshape(rows, heads, head_size)
    delta = jnp.einsum("qhd,qhd->hq", d_heads.astype(jnp.float32), attended_wide, precision=highest)

    def grad_step(key_start, running):
        d_query_acc, d_keyvalue, d_table = running
        scores, key_block, picks = block_scores(key_start, key_value_back[0])
        value_block = value_block_of(key_start, key_value_back[1])
        soft = jnp.exp(scores - log_total[:, :, None])
        d_probs = jnp.einsum(
            "qhd,khd->hqk", d_heads, value_block, preferred_element_type=jnp.float32
        )
        d_scores = (soft * (d_probs - delta[:, :, None])).astype(jnp.bfloat16)
        d_query_acc = d_query_acc + jnp.einsum(
            "hqk,khd->qhd", d_scores, key_block, preferred_element_type=jnp.float32
        )
        d_key_block = jnp.einsum(
            "hqk,qhd->khd", d_scores, query_heads, preferred_element_type=jnp.float32
        ).reshape(breadth, width)
        d_value_block = jnp.einsum(
            "hqk,qhd->khd", soft.astype(jnp.bfloat16), d_heads, preferred_element_type=jnp.float32
        ).reshape(breadth, width)
        d_keyvalue = lax.dynamic_update_slice_in_dim(
            d_keyvalue, jnp.concatenate([d_key_block, d_value_block], axis=1), key_start, 0
        )
        d_table = d_table + jnp.einsum(
            "qkb,hqk->bh", picks, d_scores.astype(jnp.float32), precision=highest
        )
        return (d_query_acc, d_keyvalue, d_table)

    start_grad = (
        jnp.zeros((rows, heads, head_size), jnp.float32),
        jnp.zeros((group_tokens, 2 * width), jnp.float32),
        jnp.zeros((buckets, heads), jnp.float32),
    )
    d_query_all, d_keyvalue_all, d_table_all = visit(grad_step, start_grad)
    own_keyvalue = lax.psum_scatter(
        d_keyvalue_all.astype(jnp.bfloat16), ("ctx", "wshard"), scatter_dimension=0, tiled=True
    ).astype(jnp.float32)
    d_query = d_query_all.reshape(rows, width).astype(jnp.bfloat16)
    d_key = own_keyvalue[:, :width].astype(jnp.bfloat16)
    d_value = own_keyvalue[:, width:].astype(jnp.bfloat16)
    grad_query = weight_product(normed, d_query)
    grad_key = weight_product(normed, d_key)
    grad_value = weight_product(normed, d_value)
    d_normed = (
        backward_product(d_query, query_back)
        + backward_product(d_key, key_back)
        + backward_product(d_value, value_back)
    )
    norm_attn_back = jax.vjp(rms_norm, inputs_wide, gain_attention)[1]
    d_input_norm, grad_gain_attn = norm_attn_back(d_normed)
    input_grad_dealt = (d_residual + d_input_norm).astype(jnp.bfloat16)
    grad_table = lax.psum(d_table_all, ("group", "ctx", "wshard"))
    returned = (
        lax.all_gather(outputs_dealt, ("ctx", "wshard"), axis=0, tiled=True),
        lax.all_gather(input_grad_dealt, ("ctx", "wshard"), axis=0, tiled=True),
    )
    own_rows = lax.dynamic_slice_in_dim(inverse, first, rows, 0)
    outputs = jnp.take(returned[0], own_rows, axis=0)
    input_grad = jnp.take(returned[1], own_rows, axis=0)
    shares = (
        lax.psum_scatter(
            grad_gain_attn.astype(jnp.bfloat16), ("ctx", "wshard"), scatter_dimension=0, tiled=True
        ).astype(jnp.float32),
        lax.psum_scatter(
            grad_query.astype(jnp.bfloat16), ("ctx", "wshard"), scatter_dimension=0, tiled=True
        ).astype(jnp.float32),
        lax.psum_scatter(
            grad_key.astype(jnp.bfloat16), ("ctx", "wshard"), scatter_dimension=0, tiled=True
        ).astype(jnp.float32),
        lax.psum_scatter(
            grad_value.astype(jnp.bfloat16), ("ctx", "wshard"), scatter_dimension=0, tiled=True
        ).astype(jnp.float32),
        lax.psum_scatter(
            grad_out.astype(jnp.bfloat16), ("ctx", "wshard"), scatter_dimension=0, tiled=True
        ).astype(jnp.float32),
        lax.psum_scatter(
            grad_gain_ff.astype(jnp.bfloat16), ("ctx", "wshard"), scatter_dimension=0, tiled=True
        ).astype(jnp.float32),
        lax.psum_scatter(
            grad_gate.astype(jnp.bfloat16), ("ctx", "wshard"), scatter_dimension=0, tiled=True
        ).astype(jnp.float32),
        lax.psum_scatter(
            grad_up.astype(jnp.bfloat16), ("ctx", "wshard"), scatter_dimension=0, tiled=True
        ).astype(jnp.float32),
        lax.psum_scatter(
            grad_down.astype(jnp.bfloat16), ("ctx", "wshard"), scatter_dimension=1, tiled=True
        ).astype(jnp.float32),
    )
    totals = (
        lax.psum(shares[0].astype(jnp.bfloat16), "group").astype(jnp.float32),
        lax.psum(shares[1].astype(jnp.bfloat16), "group").astype(jnp.float32),
        lax.psum(shares[2].astype(jnp.bfloat16), "group").astype(jnp.float32),
        lax.psum(shares[3].astype(jnp.bfloat16), "group").astype(jnp.float32),
        lax.psum(shares[4].astype(jnp.bfloat16), "group").astype(jnp.float32),
        lax.psum(shares[5].astype(jnp.bfloat16), "group").astype(jnp.float32),
        lax.psum(shares[6].astype(jnp.bfloat16), "group").astype(jnp.float32),
        lax.psum(shares[7].astype(jnp.bfloat16), "group").astype(jnp.float32),
        lax.psum(shares[8].astype(jnp.bfloat16), "group").astype(jnp.float32),
    )
    return (
        outputs,
        input_grad,
        totals[0],
        totals[1],
        totals[2],
        totals[3],
        totals[4],
        grad_table,
        totals[5],
        totals[6],
        totals[7],
        totals[8],
    )


def solution(mesh):
    return jax.shard_map(
        per_device,
        mesh=mesh,
        in_specs=(
            P(("group", "ctx", "wshard"), None),
            P(("group", "ctx", "wshard"), None),
            P("group", None),
            P("group", None),
            P(),
            P("wshard", None),
            P("wshard", None),
            P("wshard", None),
            P("wshard", None),
            P(),
            P(),
            P("wshard", None),
            P("wshard", None),
            P("wshard", None),
        ),
        out_specs=(
            P(("group", "ctx", "wshard"), None),
            P(("group", "ctx", "wshard"), None),
            P(("ctx", "wshard")),
            P(("ctx", "wshard"), None),
            P(("ctx", "wshard"), None),
            P(("ctx", "wshard"), None),
            P(("ctx", "wshard"), None),
            P(),
            P(("ctx", "wshard")),
            P(("ctx", "wshard"), None),
            P(("ctx", "wshard"), None),
            P(None, ("ctx", "wshard")),
        ),
        check_vma=False,
    )
```

profile of v0, /device:TPU:0, one launch (start us, length us, event | category | flops | bytes accessed | tf_op | source)
XLA Modules:
  0.0 1275.2 jit_solution(9304477346111395155)
XLA Ops:
  9.7 13.5 %all-gather.13.cloned.1.call-done = bf16[1536,768]{1,0:T(8,128)(2,1)} async-done(((bf16[768,768]{1,0:T(8,128)(2,1)}), bf16[1536,768]{1,0:T(8,128)(2,1)}) %all-gather.13.cloned.1.call-update) | async-done | bytes 2359312 | tf_op jit(solution)/shard_map/all_gather | solution.py:62
  23.3 3.2 convolution_convert_fusion.10
  26.6 10.4 all-gather.17.cloned.1.call-done
  37.0 3.2 convolution_convert_fusion.9
  47.1 3.7 all-gather.21.cloned.1.call-done
  53.4 20.2 %all-gather.15.cloned.1.call-done = bf16[1024,768]{1,0:T(8,128)(2,1)} async-done(((bf16[256,768]{1,0:T(8,128)(2,1)}), bf16[1024,768]{1,0:T(8,128)(2,1)}) %all-gather.15.cloned.1.call-update) | async-done | bytes 1572880 | tf_op jit(solution)/shard_map/all_gather | solution.py:108
  75.3 19.9 %all-gather.19.cloned.1.call-done = bf16[1024,768]{1,0:T(8,128)(2,1)} async-done(((bf16[256,768]{1,0:T(8,128)(2,1)}), bf16[1024,768]{1,0:T(8,128)(2,1)}) %all-gather.19.cloned.1.call-update) | async-done | bytes 1572880 | tf_op jit(solution)/shard_map/all_gather | solution.py:107
  97.6 65.7 %while.51 = (s32[]{:T(128)}, f32[12,256]{1,0:T(8,128)S(1)}, f32[12,256]{1,0:T(8,128)}, s32[1024]{0:T(1024)}, s32[4]{0:T(128)}, /*index=5*/s32[]{:T(128)}, s32[]{...) while((s32[]{:T(128)}, f32[12,256]{1,0:T(8,128)S(1)}, ...), condition=%wide.region_14.15_spmd.clone, body=%wide.region_5.14_spmd.clone.sunk | while | flops 821184512 | bytes 42105104 | solution.py:142
  102.7 26.9 %conditional.9 = ((f32[12,256]{1,0:T(8,128)S(1)}, f32[12,256]{1,0:T(8,128)})) conditional(s32[]{:T(128)} %convert_element_type.489, (f32[12,256]{1,0:T(8,128)S(1)}, f32[12,256]{1,0:T(8,128)}) %tuple.152, (s32[256]{0:T(256)}, s32[]{:T(128)}, s32[1024]{0:T(1024)}, s32[4]{0:T(128)}, bf16[1024,768]{0,1:T(8,128)(2,1)S(1)}, ...), branch_computations={%region_9.9_spmd, %region_10.13_spmd} | conditional | flops 821177856 | bytes 42094376 | solution.py:135
  105.3 7.9 fusion.6
  113.2 9.2 copy.70
  124.0 4.0 fusion.123
  134.7 28.6 %conditional.9 = ((f32[12,256]{1,0:T(8,128)S(1)}, f32[12,256]{1,0:T(8,128)})) conditional(s32[]{:T(128)} %convert_element_type.489, (f32[12,256]{1,0:T(8,128)S(1)}, f32[12,256]{1,0:T(8,128)}) %tuple.152, (s32[256]{0:T(256)}, s32[]{:T(128)}, s32[1024]{0:T(1024)}, s32[4]{0:T(128)}, bf16[1024,768]{0,1:T(8,128)(2,1)S(1)}, ...), branch_computations={%region_9.9_spmd, %region_10.13_spmd} | conditional | flops 821177856 | bytes 42094376 | solution.py:135
  137.3 7.9 fusion.6
  145.2 10.2 copy.70
  157.1 4.6 fusion.123
  165.5 67.1 %while.52 = (s32[]{:T(128)}, f32[256,12,64]{0,2,1:T(8,128)}, s32[1024]{0:T(1024)}, s32[4]{0:T(128)}, s32[]{:T(128)}, /*index=5*/s32[]{:T(128)}, bf16[1024,768]{0...) while((s32[]{:T(128)}, f32[256,12,64]{0,2,1:T(8,128)}, ...), condition=%wide.region_22.23_spmd.clone, body=%wide.region_15.22_spmd.clone.sunk | while | flops 1021128704 | bytes 33284948 | solution.py:142
  171.1 28.5 %conditional.10 = (f32[256,12,64]{0,2,1:T(8,128)}) conditional(s32[]{:T(128)} %convert_element_type.491, f32[256,12,64]{0,2,1:T(8,128)} %get-tuple-element.1644, (s32[]{:T(128)}, bf16[1024,768]{0,1:T(8,128)(2,1)S(1)}, s32[256]{0:T(256)}, s32[1024]{0:T(1024)}, s32[4]{0:T(128)}, /*index=5*/bf16[1024,768]{0,1:T(8,128)(2,1)S(1)}, ...), branch_computations={%region_19.19_spmd, %region_20.21_spmd} | conditional | flops 1021122048 | bytes 33274218 | solution.py:135
  173.7 7.5 fusion.20
  181.2 9.7 copy.71
  193.1 6.5 fusion.36
  204.8 27.7 %conditional.10 = (f32[256,12,64]{0,2,1:T(8,128)}) conditional(s32[]{:T(128)} %convert_element_type.491, f32[256,12,64]{0,2,1:T(8,128)} %get-tuple-element.1644, (s32[]{:T(128)}, bf16[1024,768]{0,1:T(8,128)(2,1)S(1)}, s32[256]{0:T(256)}, s32[1024]{0:T(1024)}, s32[4]{0:T(128)}, /*index=5*/bf16[1024,768]{0,1:T(8,128)(2,1)S(1)}, ...), branch_computations={%region_19.19_spmd, %region_20.21_spmd} | conditional | flops 1021122048 | bytes 33274218 | solution.py:135
  207.3 7.2 fusion.20
  214.5 9.2 copy.71
  225.9 6.5 fusion.36
  235.1 5.3 gather_fusion.1
  244.6 10.1 fusion.125
  254.8 10.1 fusion.126
  264.9 11.3 multiply_convert_fusion
  276.1 7.9 fusion.127
  284.1 7.4 multiply_reduce_fusion
  297.1 52.5 %while.53 = (s32[]{:T(128)}, f32[256,12,64]{0,2,1:T(8,128)S(1)}, bf16[1024,1536]{0,1:T(8,128)(2,1)}, f32[32,12]{0,1:T(8,128)S(1)}, s32[1024]{0:T(1024)S(1)}, /*i...) while((s32[]{:T(128)}, f32[256,12,64]{0,2,1:T(8,128)S(1)}, ...), condition=%wide.region_33.35_spmd.clone, body=%wide.region_26.0_spmd.clone.sunk | while | flops 1737830784 | bytes 84465112 | solution.py:142
  300.8 22.6 %conditional.11 = ((f32[256,12,64]{0,2,1:T(8,128)S(1)}, bf16[1024,1536]{0,1:T(8,128)(2,1)}, f32[32,12]{0,1:T(8,128)S(1)})) conditional(s32[]{:T(128)} %convert_element_type.493, (f32[256,12,64]{0,2,1:T(8,128)S(1)}, bf16[1024,1536]{0,1:T(8,128)(2,1)}, f32[32,12]{0,1:T(8,128)S(1)}) %tuple.159, (s32[]{:T(128)}, bf16[1024,768]{0,1:T(8,128)(2,1)S(1)}, ...), branch_computations={%region_30.31_spmd, %region_31.33_spmd} | conditional | flops 1737824128 | bytes 84454296 | solution.py:135
  302.8 5.1 fusion.51
  308.2 4.8 fusion.60
  319.6 3.8 fusion.70
  326.8 22.6 %conditional.11 = ((f32[256,12,64]{0,2,1:T(8,128)S(1)}, bf16[1024,1536]{0,1:T(8,128)(2,1)}, f32[32,12]{0,1:T(8,128)S(1)})) conditional(s32[]{:T(128)} %convert_element_type.493, (f32[256,12,64]{0,2,1:T(8,128)S(1)}, bf16[1024,1536]{0,1:T(8,128)(2,1)}, f32[32,12]{0,1:T(8,128)S(1)}) %tuple.159, (s32[]{:T(128)}, bf16[1024,768]{0,1:T(8,128)(2,1)S(1)}, ...), branch_computations={%region_30.31_spmd, %region_31.33_spmd} | conditional | flops 1737824128 | bytes 84454296 | solution.py:135
  328.8 5.1 fusion.51
  334.1 4.8 fusion.60
  345.6 3.8 fusion.70
  350.7 8.7 convolution_convert_fusion
  359.4 16.2 %copy.97 = bf16[3968,1536]{0,1:T(8,128)(2,1)} copy(bf16[3968,1536]{1,0:T(8,128)(2,1)} %convolution_convert_fusion) | data formatting | bytes 24379392
  381.5 7.0 reduce-scatter.11.cloned.1.call-done
  388.5 3.3 convolution_convert_fusion.5
  391.9 3.4 convolution_convert_fusion.4
  395.4 11.9 convolution_convert_fusion.2
  407.4 8.0 convolution_convert_fusion.1
  415.5 10.8 fusion.91
  433.6 54.4 %reduce-scatter.25.cloned.1.call-done = bf16[384,3968]{1,0:T(8,128)(2,1)} async-done(((bf16[1536,3968]{1,0:T(8,128)(2,1)}), bf16[384,3968]{1,0:T(8,128)(2,1)}) %reduce-scatter.25.cloned.1.call-update) | async-done | bytes 3047440
  488.0 4.6 copy.98
  492.5 31.4 %reduce-scatter.13.cloned.1.call-done = bf16[384,768]{1,0:T(8,128)(2,1)} async-done(((bf16[1536,768]{1,0:T(8,128)(2,1)}), bf16[384,768]{1,0:T(8,128)(2,1)}) %reduce-scatter.13.cloned.1.call-update) | async-done | bytes 589840 | tf_op jit(solution)/shard_map/reduce_scatter | solution.py:270
  523.9 35.2 %reduce-scatter.19.cloned.1.call-done = bf16[192,1536]{1,0:T(8,128)(2,1)} async-done(((bf16[768,1536]{1,0:T(8,128)(2,1)}), bf16[192,1536]{1,0:T(8,128)(2,1)}) %reduce-scatter.19.cloned.1.call-update) | async-done | bytes 589840 | tf_op jit(solution)/shard_map/reduce_scatter | solution.py:279
  559.1 35.8 %reduce-scatter.15.cloned.1.call-done = bf16[384,768]{1,0:T(8,128)(2,1)} async-done(((bf16[1536,768]{1,0:T(8,128)(2,1)}), bf16[384,768]{1,0:T(8,128)(2,1)}) %reduce-scatter.15.cloned.1.call-update) | async-done | bytes 589840 | tf_op jit(solution)/shard_map/reduce_scatter | solution.py:273
  595.0 35.2 %reduce-scatter.17.cloned.1.call-done = bf16[384,768]{1,0:T(8,128)(2,1)} async-done(((bf16[1536,768]{1,0:T(8,128)(2,1)}), bf16[384,768]{1,0:T(8,128)(2,1)}) %reduce-scatter.17.cloned.1.call-update) | async-done | bytes 589840 | tf_op jit(solution)/shard_map/reduce_scatter | solution.py:276
  630.2 99.5 %reduce-scatter.21.cloned.1.call-done = bf16[384,3968]{1,0:T(8,128)(2,1)} async-done(((bf16[1536,3968]{1,0:T(8,128)(2,1)}), bf16[384,3968]{1,0:T(8,128)(2,1)}) %reduce-scatter.21.cloned.1.call-update) | async-done | bytes 3047440 | tf_op jit(solution)/shard_map/reduce_scatter | solution.py:285
  729.7 99.5 %reduce-scatter.23.cloned.1.call-done = bf16[384,3968]{1,0:T(8,128)(2,1)} async-done(((bf16[1536,3968]{1,0:T(8,128)(2,1)}), bf16[384,3968]{1,0:T(8,128)(2,1)}) %reduce-scatter.23.cloned.1.call-update) | async-done | bytes 3047440 | tf_op jit(solution)/shard_map/reduce_scatter | solution.py:288
  829.3 4.3 scatter_custom_fusion
  835.0 39.9 %psum.75 = f32[32,12]{0,1:T(8,128)} all-reduce(f32[32,12]{0,1:T(8,128)S(1)} %copy-done.48), channel_id=1, replica_groups=mesh['group'=8,'ctx'=2,'wshard'=2] {'group','ctx','wshard'}, use_global_device_ids=true, to_apply=%region_47.49 | all-reduce | flops 384 | bytes 3072 | tf_op jit(solution)/shard_map/psum | solution.py:258
  874.9 4.3 gather_fusion
  879.3 8.2 all-reduce.4
  887.7 19.8 %all-reduce.2 = (bf16[384]{0:T(512)(128)(2,1)S(1)}, bf16[384]{0:T(512)(128)(2,1)S(1)}) all-reduce(bf16[384]{0:T(512)(128)(2,1)S(1)} %dynamic-slice.2, bf16[384]{0:T(512)(128)(2,1)S(1)} %dynamic-slice.4), channel_id=1, replica_groups=mesh['group'=8,'ctx'=2,'wshard'=2] {'group'}, use_global_device_ids=true, to_apply=%region_38.40 | all-reduce | flops 768 | bytes 3072 | tf_op jit(solution)/shard_map/psum | solution.py:296
  908.6 4.3 gather_fusion.2
  914.3 337.8 %all-reduce.7.cloned.1.call-done = (bf16[384,768]{1,0:T(8,128)(2,1)}, bf16[384,768]{1,0:T(8,128)(2,1)}, bf16[384,768]{1,0:T(8,128)(2,1)}, bf16[192,1536]{1,0:T(8...) async-done(((bf16[384,768]{1,0:T(8,128)(2,1)}, bf16[384,768]{1,0:T(8,128)(2,1)}, bf16[384,768]{1,0:T(8,128)(2,1)}, ...) | async-done | bytes 11501584 | tf_op jit(solution)/shard_map/psum | solution.py:297
  1258.9 3.0 convert_element_type.380
  (308 shorter events, 111.7 us)
Async XLA Ops:
  7.2 2.3 copy-start.1
  7.2 16.1 %copy-start.41 = (f32[1536]{0:T(1024)S(1)}, f32[1536]{0:T(1024)}, u32[]{:S(2)}) copy-start(f32[1536]{0:T(1024)} %param.32) | copy-start | bytes 18436
  7.2 16.1 %all-gather.13.cloned.1.call-start = ((), (), s32[]{:S(2)}) async-start(), calls=%async_computation.8 | async-start | bytes 3538944 | tf_op jit(solution)/shard_map/all_gather | solution.py:62
  7.9 29.0 %all-gather.17.cloned.1.call-start = ((), (), s32[]{:S(2)}) async-start(), calls=%async_computation.10 | async-start | bytes 3538944 | tf_op jit(solution)/shard_map/all_gather | solution.py:61
  8.7 42.1 %all-gather.21.cloned.1.call-start = ((), (), s32[]{:S(2)}) async-start(), calls=%async_computation.12 | async-start | bytes 3538944 | tf_op jit(solution)/shard_map/all_gather | solution.py:60
  9.4 64.2 %all-gather.15.cloned.1.call-start = ((), (), s32[]{:S(2)}) async-start(), calls=%async_computation.9 | async-start | bytes 1966080 | tf_op jit(solution)/shard_map/all_gather | solution.py:108
  9.7 16.8 %copy-start.49 = (f32[256]{0:T(256)}, f32[256]{0:T(256)S(1)}, u32[]{:S(2)}) copy-start(f32[256]{0:T(256)S(1)} %fusion.99) | copy-start | bytes 3076
  9.7 41.0 %copy-start.44 = (f32[256]{0:T(256)}, f32[256]{0:T(256)S(1)}, u32[]{:S(2)}) copy-start(f32[256]{0:T(256)S(1)} %fusion.110) | copy-start | bytes 3076
  26.5 68.7 %all-gather.19.cloned.1.call-start = ((), (), s32[]{:S(2)}) async-start(), calls=%async_computation.11 | async-start | bytes 1966080 | tf_op jit(solution)/shard_map/all_gather | solution.py:107
  40.3 194.9 %all-gather.33.cloned.1.call-start = ((), (), s32[]{:S(2)}) async-start(), calls=%async_computation.18 | async-start | bytes 3932160 | tf_op jit(solution)/shard_map/all_gather | solution.py:98
  40.8 199.6 %all-gather.23.cloned.1.call-start = ((), (), s32[]{:S(2)}) async-start(), calls=%async_computation.13 | async-start | bytes 3538944 | tf_op jit(solution)/shard_map/all_gather | solution.py:63
  41.6 203.1 %all-gather.25.cloned.1.call-start = ((), (), s32[]{:S(2)}) async-start(), calls=%async_computation.14 | async-start | bytes 18284544 | tf_op jit(solution)/shard_map/all_gather | solution.py:64
  42.3 212.4 %all-gather.27.cloned.1.call-start = ((), (), s32[]{:S(2)}) async-start(), calls=%async_computation.15 | async-start | bytes 18284544 | tf_op jit(solution)/shard_map/all_gather | solution.py:65
  43.1 221.8 %all-gather.29.cloned.1.call-start = ((), (), s32[]{:S(2)}) async-start(), calls=%async_computation.16 | async-start | bytes 18284544 | tf_op jit(solution)/shard_map/all_gather | solution.py:66
  43.7 344.8 %reduce-scatter.11.cloned.1.call-start = ((), (), s32[]{:S(2)}) async-start(), calls=%async_computation.19 | async-start | bytes 3932160 | tf_op jit(solution)/shard_map/reduce_scatter | solution.py:241
  43.9 9.5 copy-start.32
  44.6 1.9 copy-start.36
  171.1 2.0 copy-start.37
  171.1 2.6 copy-start.22
  171.1 2.6 copy-start.43
  181.2 11.9 copy-start.28
  204.8 2.0 copy-start.37
  204.8 2.6 copy-start.22
  204.8 2.6 copy-start.43
  214.5 11.4 copy-start.28
  232.6 7.8 copy-start
  240.4 2.9 copy-start.46
  243.3 48.2 %copy-start.5 = (f32[256,1536]{1,0:T(8,128)}, f32[256,1536]{1,0:T(8,128)S(1)}, u32[]{:S(2)}) copy-start(f32[256,1536]{1,0:T(8,128)S(1)} %get-tuple-element.1288) | copy-start | bytes 4718596
  276.1 7.9 copy-start.21
  276.1 7.9 copy-start.20
  284.0 7.4 copy-start.10
  284.0 7.4 copy-start.52
  291.5 2.1 copy-start.8
  294.8 2.3 copy-start.23
  294.8 2.3 copy-start.25
  294.8 2.3 copy-start.29
  294.8 2.3 copy-start.33
  294.8 2.3 copy-start.38
  294.8 2.3 copy-start.40
  341.7 1.9 copy-start.6
  349.5 9.8 copy-start.47
  349.6 138.4 %reduce-scatter.25.cloned.1.call-start = ((), (), s32[]{:S(2)}) async-start(), calls=%async_computation.27 | async-start | bytes 15237120
  375.6 148.3 %reduce-scatter.13.cloned.1.call-start = ((), (), s32[]{:S(2)}) async-start(), calls=%async_computation.21 | async-start | bytes 2949120 | tf_op jit(solution)/shard_map/reduce_scatter | solution.py:270
  376.8 2.4 copy-start.4
  376.8 2.4 copy-start.13
  379.1 180.0 %reduce-scatter.19.cloned.1.call-start = ((), (), s32[]{:S(2)}) async-start(), calls=%async_computation.24 | async-start | bytes 2949120 | tf_op jit(solution)/shard_map/reduce_scatter | solution.py:279
  381.4 213.5 %reduce-scatter.15.cloned.1.call-start = ((), (), s32[]{:S(2)}) async-start(), calls=%async_computation.22 | async-start | bytes 2949120 | tf_op jit(solution)/shard_map/reduce_scatter | solution.py:273
  391.8 3.6 copy-start.9
  391.8 238.4 %reduce-scatter.17.cloned.1.call-start = ((), (), s32[]{:S(2)}) async-start(), calls=%async_computation.23 | async-start | bytes 2949120 | tf_op jit(solution)/shard_map/reduce_scatter | solution.py:276
  395.3 334.4 %reduce-scatter.21.cloned.1.call-start = ((), (), s32[]{:S(2)}) async-start(), calls=%async_computation.25 | async-start | bytes 15237120 | tf_op jit(solution)/shard_map/reduce_scatter | solution.py:285
  407.4 421.9 %reduce-scatter.23.cloned.1.call-start = ((), (), s32[]{:S(2)}) async-start(), calls=%async_computation.26 | async-start | bytes 15237120 | tf_op jit(solution)/shard_map/reduce_scatter | solution.py:288
  415.5 459.4 %all-gather.31.cloned.1.call-start = ((), (), s32[]{:S(2)}) async-start(), calls=%async_computation.17 | async-start | bytes 3932160 | tf_op jit(solution)/shard_map/all_gather | solution.py:260
  426.3 2.9 copy-start.14
  426.3 482.3 %all-gather.35.cloned.1.call-start = ((), (), s32[]{:S(2)}) async-start(), calls=%async_computation.20 | async-start | bytes 3932160 | tf_op jit(solution)/shard_map/all_gather | solution.py:261
  426.6 2.7 copy-start.19
  433.5 818.5 %all-reduce.7.cloned.1.call-start = ((), (), s32[]{:S(2)}) async-start(), calls=%async_computation.28 | async-start | bytes 23003136 | tf_op jit(solution)/shard_map/psum | solution.py:297
  829.2 4.4 copy-start.55
  829.2 5.7 copy-start.48
  874.9 4.3 copy-start.51
  1252.1 4.6 copy-start.31
  1252.1 5.7 copy-start.30
  1254.3 4.5 copy-start.17
  1258.9 3.1 copy-start.16
  1262.0 3.1 copy-start.15
  (24 other events, 25.3 us)
Sparse Core Ops, SparseCore 0:
  9.5 13.6 all-gather.12
  24.8 12.1 all-gather.16
  38.5 12.1 all-gather.20
  52.7 20.8 all-gather.14
  75.6 19.6 all-gather.18
  96.6 28.4 all-gather.32
  126.7 10.9 all-gather.22
  139.3 25.4 all-gather.24
  166.3 25.4 all-gather.26
  193.3 25.5 all-gather.28
  349.7 38.6 reduce-scatter.10
  390.9 96.9 reduce-scatter.24
  491.1 32.8 reduce-scatter.12
  526.3 32.8 reduce-scatter.18
  562.1 32.8 reduce-scatter.14
  597.3 32.8 reduce-scatter.16
  632.6 97.0 reduce-scatter.20
  732.2 97.0 reduce-scatter.22
  831.4 29.0 all-gather.30
  862.4 29.0 all-gather.34
  897.7 354.3 all-reduce.6
where the time goes:
time: 1290 us; the launch traced here: 1280 us
  waiting for transfers between devices  809 us (63%)
  matrix products  202 us (16%)
  local copies, waits for them, and re-layouts  113 us (9%)
  blocking collectives  67.9 us (5%)
  other arithmetic  49.9 us (4%)
  loops' own time  16.9 us (1%)
  between operations  15.8 us (1%)
    psum x1, waiting for transfers between devices, per_device(): lax.psum(shares[1].astype(jnp.bfloat16), 'group').astype(jnp.float32)  338 us
    reduce_scatter x1, waiting for transfers between devices, per_device(): lax.psum_scatter(grad_up.astype(jnp.bfloat16), ('ctx', 'wshard'), scatter...  99.5 us
    reduce_scatter x1, waiting for transfers between devices, per_device(): lax.psum_scatter(grad_gate.astype(jnp.bfloat16), ('ctx', 'wshard'), scatt...  99.5 us
    unnamed x22, waiting for transfers between devices  59.8 us
    dot_general x7, matrix products, forward_product(): return jnp.dot(left_side, right_side, preferred_element_type=jnp.float32)  42.8 us
    dot_general x6, matrix products, block_scores(): jnp.einsum('qkb,bh->hqk', picks, bucket_bias, precision=highest)  40.7 us
    psum x1, blocking collectives, per_device(): grad_table = lax.psum(d_table_all, ('group', 'ctx', 'wshard'))  39.9 us
    dot_general x7, matrix products, weight_product(): lax.dot_general(left_side, right_side, (((0,), (0,)), ((), ())), preferre...  39.9 us
  transfers between devices with their start and end apart: 21, of which 14 were waited for; matrix products, arithmetic and copies ran while one was open for 21% of the time, Pallas kernels for 0%

commit v1 on v0

--- a/solution.py
+++ b/solution.py
@@ -294,7 +294,9 @@
     )
     totals = (
         lax.psum(shares[0].astype(jnp.bfloat16), "group").astype(jnp.float32),
-        lax.psum(shares[1].astype(jnp.bfloat16), "group").astype(jnp.float32),
+        jnp.sum(lax.all_gather(shares[1].astype(jnp.bfloat16), "group"), axis=0).astype(
+            jnp.float32
+        ),
         lax.psum(shares[2].astype(jnp.bfloat16), "group").astype(jnp.float32),
         lax.psum(shares[3].astype(jnp.bfloat16), "group").astype(jnp.float32),
         lax.psum(shares[4].astype(jnp.bfloat16), "group").astype(jnp.float32),

time: 1290 us -> 1350 us (1.047)
  waiting for transfers between devices: 809 us -> 873 us
    all_gather x0 -> x1, waiting for transfers between devices: none -> 58.3 us  [per_device(): lax.all_gather(shares[1].astype(jnp.bfloat16), 'group')]
    unnamed x22 -> x23, waiting for transfers between devices: 59.8 us -> 101 us
    reduce_scatter x1, waiting for transfers between devices: 31.4 us -> 0.02 us  [per_device(): lax.psum_scatter(grad_query.astype(jnp.bfloat16), ('ctx', 'wshard'), scat...]
    unnamed x97 -> x95, local copies, waits for them, and re-layouts: 30.5 us -> 30.5 us
  transfers between devices with their start and end apart: 21 -> 22, of which waited for: 14 -> 14; matrix products, arithmetic and copies ran while one was open for 21% -> 20% of each run, Pallas kernels for 0% -> 0%
where the time goes in v1:
time: 1350 us; the launch traced here: 1340 us
  waiting for transfers between devices  873 us (65%)
  matrix products  197 us (15%)
  local copies, waits for them, and re-layouts  113 us (8%)
  blocking collectives  68.2 us (5%)
  other arithmetic  53.2 us (4%)
  loops' own time  17 us (1%)
  between operations  15.9 us (1%)
    psum x1, waiting for transfers between devices, per_device(): lax.psum(shares[2].astype(jnp.bfloat16), 'group').astype(jnp.float32)  338 us
    unnamed x23, waiting for transfers between devices  101 us
    reduce_scatter x1, waiting for transfers between devices, per_device(): lax.psum_scatter(grad_gate.astype(jnp.bfloat16), ('ctx', 'wshard'), scatt...  99.5 us
    reduce_scatter x1, waiting for transfers between devices, per_device(): lax.psum_scatter(grad_up.astype(jnp.bfloat16), ('ctx', 'wshard'), scatter...  99.5 us
    all_gather x1, waiting for transfers between devices, per_device(): lax.all_gather(shares[1].astype(jnp.bfloat16), 'group')  58.3 us
    dot_general x7, matrix products, forward_product(): return jnp.dot(left_side, right_side, preferred_element_type=jnp.float32)  41.8 us
    dot_general x6, matrix products, block_scores(): jnp.einsum('qkb,bh->hqk', picks, bucket_bias, precision=highest)  40.7 us
    psum x1, blocking collectives, per_device(): grad_table = lax.psum(d_table_all, ('group', 'ctx', 'wshard'))  39.9 us
  transfers between devices with their start and end apart: 22, of which 14 were waited for; matrix products, arithmetic and copies ran while one was open for 20% of the time, Pallas kernels for 0%

profile of v1, /device:TPU:0, one launch (start us, length us, event | category | flops | bytes accessed | tf_op | source)
XLA Modules:
  0.0 1337.5 jit_solution(5522717260750364298)
XLA Ops:
  9.7 13.5 %all-gather.15.cloned.1.call-done = bf16[1536,768]{1,0:T(8,128)(2,1)} async-done(((bf16[768,768]{1,0:T(8,128)(2,1)}), bf16[1536,768]{1,0:T(8,128)(2,1)}) %all-gather.15.cloned.1.call-update) | async-done | bytes 2359312 | tf_op jit(solution)/shard_map/all_gather | solution.py:62
  23.3 3.2 convolution_convert_fusion.10
  26.6 10.4 all-gather.19.cloned.1.call-done
  37.0 3.2 convolution_convert_fusion.9
  47.1 3.6 all-gather.23.cloned.1.call-done
  53.4 20.2 %all-gather.17.cloned.1.call-done = bf16[1024,768]{1,0:T(8,128)(2,1)} async-done(((bf16[256,768]{1,0:T(8,128)(2,1)}), bf16[1024,768]{1,0:T(8,128)(2,1)}) %all-gather.17.cloned.1.call-update) | async-done | bytes 1572880 | tf_op jit(solution)/shard_map/all_gather | solution.py:108
  75.3 19.9 %all-gather.21.cloned.1.call-done = bf16[1024,768]{1,0:T(8,128)(2,1)} async-done(((bf16[256,768]{1,0:T(8,128)(2,1)}), bf16[1024,768]{1,0:T(8,128)(2,1)}) %all-gather.21.cloned.1.call-update) | async-done | bytes 1572880 | tf_op jit(solution)/shard_map/all_gather | solution.py:107
  97.6 65.7 %while.51 = (s32[]{:T(128)}, f32[12,256]{1,0:T(8,128)S(1)}, f32[12,256]{1,0:T(8,128)}, s32[1024]{0:T(1024)}, s32[4]{0:T(128)}, /*index=5*/s32[]{:T(128)}, s32[]{...) while((s32[]{:T(128)}, f32[12,256]{1,0:T(8,128)S(1)}, ...), condition=%wide.region_14.15_spmd.clone, body=%wide.region_5.14_spmd.clone.sunk | while | flops 821184512 | bytes 42105104 | solution.py:142
  102.7 26.8 %conditional.9 = ((f32[12,256]{1,0:T(8,128)S(1)}, f32[12,256]{1,0:T(8,128)})) conditional(s32[]{:T(128)} %convert_element_type.491, (f32[12,256]{1,0:T(8,128)S(1)}, f32[12,256]{1,0:T(8,128)}) %tuple.152, (s32[256]{0:T(256)}, s32[]{:T(128)}, s32[1024]{0:T(1024)}, s32[4]{0:T(128)}, bf16[1024,768]{0,1:T(8,128)(2,1)S(1)}, ...), branch_computations={%region_9.9_spmd, %region_10.13_spmd} | conditional | flops 821177856 | bytes 42094376 | solution.py:135
  105.3 7.9 fusion.6
  113.2 9.2 copy.70
  124.0 4.0 fusion.123
  134.7 28.5 %conditional.9 = ((f32[12,256]{1,0:T(8,128)S(1)}, f32[12,256]{1,0:T(8,128)})) conditional(s32[]{:T(128)} %convert_element_type.491, (f32[12,256]{1,0:T(8,128)S(1)}, f32[12,256]{1,0:T(8,128)}) %tuple.152, (s32[256]{0:T(256)}, s32[]{:T(128)}, s32[1024]{0:T(1024)}, s32[4]{0:T(128)}, bf16[1024,768]{0,1:T(8,128)(2,1)S(1)}, ...), branch_computations={%region_9.9_spmd, %region_10.13_spmd} | conditional | flops 821177856 | bytes 42094376 | solution.py:135
  137.3 7.9 fusion.6
  145.2 10.2 copy.70
  157.0 4.7 fusion.123
  165.5 67.3 %while.52 = (s32[]{:T(128)}, f32[256,12,64]{0,2,1:T(8,128)}, s32[1024]{0:T(1024)}, s32[4]{0:T(128)}, s32[]{:T(128)}, /*index=5*/s32[]{:T(128)}, bf16[1024,768]{0...) while((s32[]{:T(128)}, f32[256,12,64]{0,2,1:T(8,128)}, ...), condition=%wide.region_22.23_spmd.clone, body=%wide.region_15.22_spmd.clone.sunk | while | flops 1021128704 | bytes 33284948 | solution.py:142
  171.2 28.5 %conditional.10 = (f32[256,12,64]{0,2,1:T(8,128)}) conditional(s32[]{:T(128)} %convert_element_type.493, f32[256,12,64]{0,2,1:T(8,128)} %get-tuple-element.1643, (s32[]{:T(128)}, bf16[1024,768]{0,1:T(8,128)(2,1)S(1)}, s32[256]{0:T(256)}, s32[1024]{0:T(1024)}, s32[4]{0:T(128)}, /*index=5*/bf16[1024,768]{0,1:T(8,128)(2,1)S(1)}, ...), branch_computations={%region_19.19_spmd, %region_20.21_spmd} | conditional | flops 1021122048 | bytes 33274218 | solution.py:135
  173.8 7.5 fusion.20
  181.3 9.7 copy.71
  193.2 6.5 fusion.36
  205.0 27.7 %conditional.10 = (f32[256,12,64]{0,2,1:T(8,128)}) conditional(s32[]{:T(128)} %convert_element_type.493, f32[256,12,64]{0,2,1:T(8,128)} %get-tuple-element.1643, (s32[]{:T(128)}, bf16[1024,768]{0,1:T(8,128)(2,1)S(1)}, s32[256]{0:T(256)}, s32[1024]{0:T(1024)}, s32[4]{0:T(128)}, /*index=5*/bf16[1024,768]{0,1:T(8,128)(2,1)S(1)}, ...), branch_computations={%region_19.19_spmd, %region_20.21_spmd} | conditional | flops 1021122048 | bytes 33274218 | solution.py:135
  207.5 7.2 fusion.20
  214.7 9.2 copy.71
  226.1 6.5 fusion.36
  235.3 5.3 gather_fusion.1
  244.8 10.1 fusion.125
  254.9 10.1 fusion.126
  265.1 11.3 multiply_convert_fusion
  276.3 7.9 fusion.127
  284.2 7.4 multiply_reduce_fusion
  297.3 52.5 %while.53 = (s32[]{:T(128)}, f32[256,12,64]{0,2,1:T(8,128)S(1)}, bf16[1024,1536]{0,1:T(8,128)(2,1)}, f32[32,12]{0,1:T(8,128)S(1)}, s32[1024]{0:T(1024)S(1)}, /*i...) while((s32[]{:T(128)}, f32[256,12,64]{0,2,1:T(8,128)S(1)}, ...), condition=%wide.region_33.35_spmd.clone, body=%wide.region_26.0_spmd.clone.sunk | while | flops 1737830784 | bytes 84465112 | solution.py:142
  301.0 22.6 %conditional.11 = ((f32[256,12,64]{0,2,1:T(8,128)S(1)}, bf16[1024,1536]{0,1:T(8,128)(2,1)}, f32[32,12]{0,1:T(8,128)S(1)})) conditional(s32[]{:T(128)} %convert_element_type.495, (f32[256,12,64]{0,2,1:T(8,128)S(1)}, bf16[1024,1536]{0,1:T(8,128)(2,1)}, f32[32,12]{0,1:T(8,128)S(1)}) %tuple.159, (s32[]{:T(128)}, bf16[1024,768]{0,1:T(8,128)(2,1)S(1)}, ...), branch_computations={%region_30.31_spmd, %region_31.33_spmd} | conditional | flops 1737824128 | bytes 84454296 | solution.py:135
  303.0 5.1 fusion.51
  308.4 4.8 fusion.60
  319.8 3.8 fusion.70
  327.0 22.6 %conditional.11 = ((f32[256,12,64]{0,2,1:T(8,128)S(1)}, bf16[1024,1536]{0,1:T(8,128)(2,1)}, f32[32,12]{0,1:T(8,128)S(1)})) conditional(s32[]{:T(128)} %convert_element_type.495, (f32[256,12,64]{0,2,1:T(8,128)S(1)}, bf16[1024,1536]{0,1:T(8,128)(2,1)}, f32[32,12]{0,1:T(8,128)S(1)}) %tuple.159, (s32[]{:T(128)}, bf16[1024,768]{0,1:T(8,128)(2,1)S(1)}, ...), branch_computations={%region_30.31_spmd, %region_31.33_spmd} | conditional | flops 1737824128 | bytes 84454296 | solution.py:135
  328.9 5.1 fusion.51
  334.3 4.8 fusion.60
  345.8 3.8 fusion.70
  353.3 8.4 convolution_convert_fusion
  361.7 15.9 %copy.97 = bf16[3968,1536]{0,1:T(8,128)(2,1)} copy(bf16[3968,1536]{1,0:T(8,128)(2,1)} %convolution_convert_fusion) | data formatting | bytes 24379392
  381.4 7.2 reduce-scatter.11.cloned.1.call-done
  388.6 3.3 convolution_convert_fusion.5
  392.0 3.4 convolution_convert_fusion.4
  395.5 8.0 convolution_convert_fusion.2
  403.6 7.9 convolution_convert_fusion.1
  411.6 9.8 fusion.91
  429.4 94.7 %reduce-scatter.25.cloned.1.call-done = bf16[384,3968]{1,0:T(8,128)(2,1)} async-done(((bf16[1536,3968]{1,0:T(8,128)(2,1)}), bf16[384,3968]{1,0:T(8,128)(2,1)}) %reduce-scatter.25.cloned.1.call-update) | async-done | bytes 3047440
  524.1 4.6 copy.98
  528.6 30.7 %reduce-scatter.19.cloned.1.call-done = bf16[192,1536]{1,0:T(8,128)(2,1)} async-done(((bf16[768,1536]{1,0:T(8,128)(2,1)}), bf16[192,1536]{1,0:T(8,128)(2,1)}) %reduce-scatter.19.cloned.1.call-update) | async-done | bytes 589840 | tf_op jit(solution)/shard_map/reduce_scatter | solution.py:279
  559.3 35.8 %reduce-scatter.15.cloned.1.call-done = bf16[384,768]{1,0:T(8,128)(2,1)} async-done(((bf16[1536,768]{1,0:T(8,128)(2,1)}), bf16[384,768]{1,0:T(8,128)(2,1)}) %reduce-scatter.15.cloned.1.call-update) | async-done | bytes 589840 | tf_op jit(solution)/shard_map/reduce_scatter | solution.py:273
  595.1 35.2 %reduce-scatter.17.cloned.1.call-done = bf16[384,768]{1,0:T(8,128)(2,1)} async-done(((bf16[1536,768]{1,0:T(8,128)(2,1)}), bf16[384,768]{1,0:T(8,128)(2,1)}) %reduce-scatter.17.cloned.1.call-update) | async-done | bytes 589840 | tf_op jit(solution)/shard_map/reduce_scatter | solution.py:276
  630.3 99.5 %reduce-scatter.21.cloned.1.call-done = bf16[384,3968]{1,0:T(8,128)(2,1)} async-done(((bf16[1536,3968]{1,0:T(8,128)(2,1)}), bf16[384,3968]{1,0:T(8,128)(2,1)}) %reduce-scatter.21.cloned.1.call-update) | async-done | bytes 3047440 | tf_op jit(solution)/shard_map/reduce_scatter | solution.py:285
  729.8 99.5 %reduce-scatter.23.cloned.1.call-done = bf16[384,3968]{1,0:T(8,128)(2,1)} async-done(((bf16[1536,3968]{1,0:T(8,128)(2,1)}), bf16[384,3968]{1,0:T(8,128)(2,1)}) %reduce-scatter.23.cloned.1.call-update) | async-done | bytes 3047440 | tf_op jit(solution)/shard_map/reduce_scatter | solution.py:288
  829.4 4.3 scatter_custom_fusion
  835.1 39.9 %psum.67 = f32[32,12]{0,1:T(8,128)} all-reduce(f32[32,12]{0,1:T(8,128)S(1)} %copy-done.47), channel_id=1, replica_groups=mesh['group'=8,'ctx'=2,'wshard'=2] {'group','ctx','wshard'}, use_global_device_ids=true, to_apply=%region_47.49 | all-reduce | flops 384 | bytes 3072 | tf_op jit(solution)/shard_map/psum | solution.py:258
  875.0 4.3 gather_fusion
  879.3 8.2 all-reduce.4
  887.7 20.0 %all-reduce.2 = (bf16[384]{0:T(512)(128)(2,1)S(1)}, bf16[384]{0:T(512)(128)(2,1)S(1)}) all-reduce(bf16[384]{0:T(512)(128)(2,1)S(1)} %dynamic-slice.2, bf16[384]{0:T(512)(128)(2,1)S(1)} %dynamic-slice.4), channel_id=1, replica_groups=mesh['group'=8,'ctx'=2,'wshard'=2] {'group'}, use_global_device_ids=true, to_apply=%region_38.40 | all-reduce | flops 768 | bytes 3072 | tf_op jit(solution)/shard_map/psum | solution.py:296
  909.0 4.3 gather_fusion.2
  914.6 58.3 %all-gather.39.cloned.1.call-done = bf16[3072,768]{1,0:T(8,128)(2,1)} async-done(((bf16[384,768]{1,0:T(8,128)(2,1)}), bf16[3072,768]{1,0:T(8,128)(2,1)}) %all-gather.39.cloned.1.call-update) | async-done | bytes 4718608 | tf_op jit(solution)/shard_map/all_gather | solution.py:297
  972.9 3.3 reduce_sum.180
  977.3 338.3 %all-reduce.7.cloned.1.call-done = (bf16[384,768]{1,0:T(8,128)(2,1)}, bf16[384,768]{1,0:T(8,128)(2,1)}, bf16[192,1536]{1,0:T(8,128)(2,1)}, bf16[384,3968]{1,0:T(...) async-done(((bf16[384,768]{1,0:T(8,128)(2,1)}, bf16[384,768]{1,0:T(8,128)(2,1)}, bf16[192,1536]{1,0:T(8,128)(2,1)}, bf16[384,3968]{1,0:T(8,128)(2,1)}, ...) | async-done | bytes 10911760 | tf_op jit(solution)/shard_map/psum | solution.py:300
  (310 shorter events, 115.8 us)
Async XLA Ops:
  7.2 2.3 copy-start.1
  7.2 16.1 %copy-start.40 = (f32[1536]{0:T(1024)S(1)}, f32[1536]{0:T(1024)}, u32[]{:S(2)}) copy-start(f32[1536]{0:T(1024)} %param.32) | copy-start | bytes 18436
  7.2 16.1 %all-gather.15.cloned.1.call-start = ((), (), s32[]{:S(2)}) async-start(), calls=%async_computation.8 | async-start | bytes 3538944 | tf_op jit(solution)/shard_map/all_gather | solution.py:62
  7.9 29.0 %all-gather.19.cloned.1.call-start = ((), (), s32[]{:S(2)}) async-start(), calls=%async_computation.10 | async-start | bytes 3538944 | tf_op jit(solution)/shard_map/all_gather | solution.py:61
  8.7 42.1 %all-gather.23.cloned.1.call-start = ((), (), s32[]{:S(2)}) async-start(), calls=%async_computation.12 | async-start | bytes 3538944 | tf_op jit(solution)/shard_map/all_gather | solution.py:60
  9.4 64.2 %all-gather.17.cloned.1.call-start = ((), (), s32[]{:S(2)}) async-start(), calls=%async_computation.9 | async-start | bytes 1966080 | tf_op jit(solution)/shard_map/all_gather | solution.py:108
  9.7 16.8 %copy-start.48 = (f32[256]{0:T(256)}, f32[256]{0:T(256)S(1)}, u32[]{:S(2)}) copy-start(f32[256]{0:T(256)S(1)} %fusion.99) | copy-start | bytes 3076
  9.7 41.0 %copy-start.43 = (f32[256]{0:T(256)}, f32[256]{0:T(256)S(1)}, u32[]{:S(2)}) copy-start(f32[256]{0:T(256)S(1)} %fusion.110) | copy-start | bytes 3076
  26.6 68.7 %all-gather.21.cloned.1.call-start = ((), (), s32[]{:S(2)}) async-start(), calls=%async_computation.11 | async-start | bytes 1966080 | tf_op jit(solution)/shard_map/all_gather | solution.py:107
  40.2 195.1 %all-gather.35.cloned.1.call-start = ((), (), s32[]{:S(2)}) async-start(), calls=%async_computation.18 | async-start | bytes 3932160 | tf_op jit(solution)/shard_map/all_gather | solution.py:98
  40.8 199.8 %all-gather.25.cloned.1.call-start = ((), (), s32[]{:S(2)}) async-start(), calls=%async_computation.13 | async-start | bytes 3538944 | tf_op jit(solution)/shard_map/all_gather | solution.py:63
  41.6 203.3 %all-gather.27.cloned.1.call-start = ((), (), s32[]{:S(2)}) async-start(), calls=%async_computation.14 | async-start | bytes 18284544 | tf_op jit(solution)/shard_map/all_gather | solution.py:64
  42.3 212.6 %all-gather.29.cloned.1.call-start = ((), (), s32[]{:S(2)}) async-start(), calls=%async_computation.15 | async-start | bytes 18284544 | tf_op jit(solution)/shard_map/all_gather | solution.py:65
  43.1 222.0 %all-gather.31.cloned.1.call-start = ((), (), s32[]{:S(2)}) async-start(), calls=%async_computation.16 | async-start | bytes 18284544 | tf_op jit(solution)/shard_map/all_gather | solution.py:66
  43.7 344.9 %reduce-scatter.11.cloned.1.call-start = ((), (), s32[]{:S(2)}) async-start(), calls=%async_computation.19 | async-start | bytes 3932160 | tf_op jit(solution)/shard_map/reduce_scatter | solution.py:241
  43.9 9.5 copy-start.31
  44.6 2.0 copy-start.35
  171.2 2.0 copy-start.36
  171.2 2.6 copy-start.22
  171.2 2.6 copy-start.42
  181.3 11.9 copy-start.28
  205.0 2.0 copy-start.36
  205.0 2.6 copy-start.22
  205.0 2.6 copy-start.42
  214.7 11.4 copy-start.28
  232.8 7.8 copy-start
  240.6 2.9 copy-start.45
  243.5 48.2 %copy-start.5 = (f32[256,1536]{1,0:T(8,128)}, f32[256,1536]{1,0:T(8,128)S(1)}, u32[]{:S(2)}) copy-start(f32[256,1536]{1,0:T(8,128)S(1)} %get-tuple-element.1287) | copy-start | bytes 4718596
  276.3 7.9 copy-start.21
  276.3 7.9 copy-start.20
  284.2 7.4 copy-start.10
  284.2 7.4 copy-start.51
  291.7 2.1 copy-start.8
  294.9 2.3 copy-start.23
  294.9 2.3 copy-start.25
  294.9 2.3 copy-start.29
  294.9 2.3 copy-start.32
  294.9 2.3 copy-start.37
  295.0 2.3 copy-start.39
  316.0 1.9 copy-start.6
  341.9 1.9 copy-start.6
  349.8 78.9 %reduce-scatter.13.cloned.1.call-start = ((), (), s32[]{:S(2)}) async-start(), calls=%async_computation.21 | async-start | bytes 2949120 | tf_op jit(solution)/shard_map/reduce_scatter | solution.py:270
  350.9 2.4 copy-start.11
  350.9 2.4 copy-start.52
  353.3 170.8 %reduce-scatter.25.cloned.1.call-start = ((), (), s32[]{:S(2)}) async-start(), calls=%async_computation.28 | async-start | bytes 15237120
  377.7 181.6 %reduce-scatter.19.cloned.1.call-start = ((), (), s32[]{:S(2)}) async-start(), calls=%async_computation.24 | async-start | bytes 2949120 | tf_op jit(solution)/shard_map/reduce_scatter | solution.py:279
  381.3 213.7 %reduce-scatter.15.cloned.1.call-start = ((), (), s32[]{:S(2)}) async-start(), calls=%async_computation.22 | async-start | bytes 2949120 | tf_op jit(solution)/shard_map/reduce_scatter | solution.py:273
  391.9 3.6 copy-start.9
  391.9 238.4 %reduce-scatter.17.cloned.1.call-start = ((), (), s32[]{:S(2)}) async-start(), calls=%async_computation.23 | async-start | bytes 2949120 | tf_op jit(solution)/shard_map/reduce_scatter | solution.py:276
  395.4 334.4 %reduce-scatter.21.cloned.1.call-start = ((), (), s32[]{:S(2)}) async-start(), calls=%async_computation.25 | async-start | bytes 15237120 | tf_op jit(solution)/shard_map/reduce_scatter | solution.py:285
  403.5 425.8 %reduce-scatter.23.cloned.1.call-start = ((), (), s32[]{:S(2)}) async-start(), calls=%async_computation.26 | async-start | bytes 15237120 | tf_op jit(solution)/shard_map/reduce_scatter | solution.py:288
  411.5 463.5 %all-gather.33.cloned.1.call-start = ((), (), s32[]{:S(2)}) async-start(), calls=%async_computation.17 | async-start | bytes 3932160 | tf_op jit(solution)/shard_map/all_gather | solution.py:260
  421.4 2.9 copy-start.14
  421.4 487.6 %all-gather.37.cloned.1.call-start = ((), (), s32[]{:S(2)}) async-start(), calls=%async_computation.20 | async-start | bytes 3932160 | tf_op jit(solution)/shard_map/all_gather | solution.py:261
  421.6 2.7 copy-start.19
  428.6 544.3 %all-gather.39.cloned.1.call-start = ((), (), s32[]{:S(2)}) async-start(), calls=%async_computation.27 | async-start | bytes 5308416 | tf_op jit(solution)/shard_map/all_gather | solution.py:297
  429.3 886.2 %all-reduce.7.cloned.1.call-start = ((), (), s32[]{:S(2)}) async-start(), calls=%async_computation.29 | async-start | bytes 21823488 | tf_op jit(solution)/shard_map/psum | solution.py:300
  829.3 4.4 copy-start.54
  829.3 5.7 copy-start.47
  875.0 4.3 copy-start.50
  1315.5 4.5 copy-start.30
  1315.5 5.6 copy-start.17
  1321.1 3.1 copy-start.16
  1324.3 3.1 copy-start.15
  (24 other events, 24.5 us)
Sparse Core Ops, SparseCore 0:
  9.5 13.6 all-gather.14
  24.8 12.1 all-gather.18
  38.5 12.1 all-gather.22
  52.7 20.8 all-gather.16
  75.6 19.6 all-gather.20
  96.6 28.4 all-gather.34
  126.7 10.9 all-gather.24
  139.3 25.4 all-gather.26
  166.3 25.5 all-gather.28
  193.3 25.4 all-gather.30
  349.9 38.6 reduce-scatter.10
  391.5 32.8 reduce-scatter.12
  427.0 96.9 reduce-scatter.24
  526.4 32.8 reduce-scatter.18
  562.3 32.7 reduce-scatter.14
  597.5 32.8 reduce-scatter.16
  632.8 97.0 reduce-scatter.20
  732.3 96.9 reduce-scatter.22
  831.5 29.0 all-gather.32
  862.5 29.1 all-gather.36
  893.8 78.9 all-gather.38
  978.7 336.7 all-reduce.6
